TPU v7x, 32 devices: a whole 2x2x4 slice. The times are simulated.
32 devices in a mesh: groups: 2 (over x), seq: 16 (over z, y, core).
Axes of the slice: x: 2, y: 2, z: 4, core: 2. Of those that a mesh axis runs over, the one named last changes fastest.
Arguments:
- clip_tokens: bfloat16 [32, 128, 512], P(('groups', 'seq')), parts along dimension 0, may hold values from -6 to 6
- spatial_qkv: bfloat16 [512, 1536], replicated, may hold values from -4.6403883 to 4.6403883
- spatial_out: bfloat16 [512, 512], replicated, may hold values from -0.5 to 0.5
- temporal_qkv: bfloat16 [512, 1536], replicated, may hold values from -4.6403883 to 4.6403883
- temporal_out: bfloat16 [512, 512], replicated, may hold values from -0.5 to 0.5
- mlp_up: bfloat16 [512, 2048], replicated, may hold values from -0.25 to 0.25
- mlp_down: bfloat16 [2048, 512], replicated, may hold values from -0.25 to 0.25
Outputs:
- layer_out: bfloat16 [32, 128, 512], P(('groups', 'seq')), parts along dimension 0
There are 2 independent parts, one for each index of `groups`. A program takes and returns all parts, laid end to end along the dimension named above; an argument that names none is the same for every part. Nothing has to cross between parts.
All inputs are finite; a program needn't handle non-finite values.
Results may differ from a plain program's by a relative error of at most 0.013.
Values may be sent and summed in bfloat16 or wider, within the bound.
A program may use at most 128 MiB of HBM per device.

v0:
```python
import jax
import jax.numpy as jnp
from jax import lax
from jax.sharding import PartitionSpec as P

HEADS = 8


def norm_rows(values):
    center = values - jnp.mean(values, axis=-1, keepdims=True)
    spread = jnp.mean(center * center, axis=-1, keepdims=True)
    return (center * lax.rsqrt(spread + 1e-05)).astype(jnp.bfloat16)


def softmax_rows(scores):
    row_max = jnp.max(scores, axis=-1, keepdims=True)
    raised = jnp.exp(scores - row_max)
    return (raised / jnp.sum(raised, axis=-1, keepdims=True)).astype(jnp.bfloat16)


def spatial_frame(frame_rows, w_qkv, w_out):
    patches, model_width = frame_rows.shape
    head_width = model_width // HEADS
    packed = jnp.dot(
        norm_rows(frame_rows.astype(jnp.float32)), w_qkv, preferred_element_type=jnp.float32
    )
    packed = packed.astype(jnp.bfloat16).reshape(patches, 3, HEADS, head_width)
    key_rows = packed[:, 1]
    value_rows = packed[:, 2]
    block_rows = min(512, patches)
    query_rows = packed[:, 0].reshape(patches // block_rows, block_rows, HEADS, head_width)

    def one_block(query_block):
        scores = jnp.einsum(
            "qhd,khd->hqk", query_block, key_rows, preferred_element_type=jnp.float32
        ) * head_width ** (-0.5)
        weights = softmax_rows(scores)
        attended = jnp.einsum(
            "hqk,khd->qhd", weights, value_rows, preferred_element_type=jnp.float32
        )
        return attended.astype(jnp.bfloat16).reshape(block_rows, model_width)

    attended = lax.map(one_block, query_rows).reshape(patches, model_width)
    merged = frame_rows.astype(jnp.float32) + jnp.dot(
        attended, w_out, preferred_element_type=jnp.float32
    )
    return merged.astype(jnp.bfloat16)


def temporal_block(tokens, w_qkv, w_out):
    frames, count_rows, model_width = tokens.shape
    head_width = model_width // HEADS
    flat_rows = tokens.reshape(frames * count_rows, model_width)
    packed = jnp.dot(
        norm_rows(flat_rows.astype(jnp.float32)), w_qkv, preferred_element_type=jnp.float32
    )
    packed = packed.astype(jnp.bfloat16).reshape(frames, count_rows, 3, HEADS, head_width)
    scores = jnp.einsum(
        "fkhd,gkhd->khfg", packed[:, :, 0], packed[:, :, 1], preferred_element_type=jnp.float32
    ) * head_width ** (-0.5)
    weights = softmax_rows(scores)
    attended = jnp.einsum(
        "khfg,gkhd->fkhd", weights, packed[:, :, 2], preferred_element_type=jnp.float32
    )
    attended = attended.astype(jnp.bfloat16).reshape(frames * count_rows, model_width)
    merged = flat_rows.astype(jnp.float32) + jnp.dot(
        attended, w_out, preferred_element_type=jnp.float32
    )
    return merged.astype(jnp.bfloat16)


def feed_forward(tokens, w_up, w_down):
    raised = jnp.dot(
        norm_rows(tokens.astype(jnp.float32)), w_up, preferred_element_type=jnp.float32
    )
    hidden = jax.nn.gelu(raised, approximate=True).astype(jnp.bfloat16)
    merged = tokens.astype(jnp.float32) + jnp.dot(
        hidden, w_down, preferred_element_type=jnp.float32
    )
    return merged.astype(jnp.bfloat16)


def local(clip_tokens, spatial_qkv, spatial_out, temporal_qkv, temporal_out, mlp_up, mlp_down):
    frame_count, patches, model_width = clip_tokens.shape
    devices = lax.axis_size("seq")
    mixed = lax.map(
        lambda frame_rows: spatial_frame(frame_rows, spatial_qkv, spatial_out), clip_tokens
    )
    blocks = mixed.reshape(frame_count, devices, patches // devices, model_width)
    arrived = lax.all_to_all(blocks, "seq", split_axis=1, concat_axis=0, tiled=True)
    frames = arrived.shape[0]
    count_rows = arrived.shape[2]
    tokens = arrived.reshape(frames, count_rows, model_width)
    after_time = temporal_block(tokens, temporal_qkv, temporal_out)
    returned = after_time.reshape(frames, 1, count_rows, model_width)
    arrived_back = lax.all_to_all(returned, "seq", split_axis=0, concat_axis=1, tiled=True)
    result_rows = arrived_back.reshape(frame_count * patches, model_width)
    result_rows = feed_forward(result_rows, mlp_up, mlp_down)
    return result_rows.reshape(frame_count, patches, model_width)


def solution(mesh):
    in_specs = (P(("groups", "seq"), None, None), P(), P(), P(), P(), P(), P())
    out_specs = P(("groups", "seq"), None, None)
    return jax.shard_map(local, mesh=mesh, in_specs=in_specs, out_specs=out_specs, check_vma=False)
```

profile of v0, /device:TPU:0, one launch (start us, length us, event | category | flops | bytes accessed | tf_op | source)
XLA Modules:
  0.0 44.1 jit_solution(6778775718888962342)
XLA Ops:
  0.0 0.0 copy-start
  0.0 1.2 %convert_reduce_fusion.2 = f32[128]{0:T(128)S(1)} fusion(bf16[1,128,512]{2,1,0:T(8,128)(2,1)} %param.7), kind=kLoop, calls=%fused_computation.45 | loop fusion | flops 130944 | bytes 131584 | tf_op jit(solution)/shard_map/while/body/eval_jaxpr/reduce_sum | solution.py:10
  1.2 1.1 %fusion.31 = f32[128]{0:T(128)S(1)} fusion(bf16[1,128,512]{2,1,0:T(8,128)(2,1)} %param.7, f32[128]{0:T(128)S(1)} %broadcast_multiply_fusion.2), kind=kLoop, calls=%fused_computation.50 | loop fusion | flops 262016 | bytes 132096 | tf_op jit(solution)/shard_map/while/body/eval_jaxpr/reduce_sum | solution.py:11
  2.3 1.9 %convolution_convert_fusion.1 = bf16[128,1536]{1,0:T(8,128)(2,1)S(1)} fusion(bf16[512,1536]{1,0:T(8,128)(2,1)} %param.8, bf16[1,128,512]{2,1,0:T(8,128)(2,1)} %param.7, f32[128]{0:T(128)S(1)} %add_rsqrt_fusion.2, f32[128]{0:T(128)S(1)} %broadcast_multiply_fusion.2), kind=kOutput, calls=%fused_computation.3 | convolution fusion | flops 201785344 | bytes 2098176 | tf_op jit(solution)/shard_map/while/body/eval_jaxpr/dot_general | solution.py:24
  4.2 0.2 copy.23
  4.4 0.0 copy-start.1
  4.4 0.0 copy-start.2
  4.4 0.4 fusion.67
  4.8 1.1 %convolution_multiply_fusion = f32[8,128,128]{1,2,0:T(8,128)} fusion(bf16[128,3,8,64]{0,3,2,1:T(8,128)(2,1)S(1)} %bitcast.104), kind=kOutput, calls=%fused_computation.9 | convolution fusion | flops 16908288 | bytes 786432 | tf_op jit(solution)/shard_map/while/body/eval_jaxpr/while/body/eval_jaxpr/qhd,khd->hqk/dot_general | solution.py:34
  5.9 1.5 %convolution_convert_fusion.3 = bf16[8,64,128]{2,1,0:T(8,128)(2,1)S(1)} fusion(f32[8,128]{1,0:T(8,128)S(1)} %fusion.67, bf16[128,3,8,64]{0,3,2,1:T(8,128)(2,1)S(1)} %bitcast.105, f32[8,128,128]{1,2,0:T(8,128)} %convolution_multiply_fusion), kind=kOutput, calls=%fused_computation.19 | convolution fusion | flops 17237120 | bytes 1314816 | tf_op jit(solution)/shard_map/while/body/eval_jaxpr/while/body/eval_jaxpr/hqk,khd->qhd/dot_general | solution.py:38
  7.4 0.0 copy-done.1
  7.4 0.0 copy-done.2
  7.4 0.3 fusion.12
  7.6 15.1 %all_to_all.8 = bf16[1,16,8,512]{3,2,0,1:T(8,128)(2,1)S(1)} all-to-all(bf16[1,16,8,512]{3,2,0,1:T(8,128)(2,1)S(1)} %fusion.12), channel_id=1, replica_groups=mesh['groups'=2,'seq'=16] {'seq'}, dimensions={1} | all-to-all | bytes 262144 | tf_op jit(solution)/shard_map/all_to_all | solution.py:90
  22.8 0.1 convert_reduce_fusion.1
  22.9 0.1 div.53
  23.0 0.2 fusion.38
  23.2 0.1 rsqrt.33
  23.2 1.8 %convolution_convert_fusion = bf16[128,1536]{1,0:T(8,128)(2,1)S(1)} fusion(bf16[512,1536]{1,0:T(8,128)(2,1)} %param.10, bf16[1,16,8,512]{3,2,0,1:T(8,128)(2,1)S(1)} %all_to_all.8, f32[128]{0:T(128)S(1)} %rsqrt.33, f32[128]{0:T(128)S(1)} %div.53), kind=kOutput, calls=%fused_computation.2 | convolution fusion | flops 201785344 | bytes 2098176 | tf_op jit(solution)/shard_map/dot_general | solution.py:54
  25.1 0.4 %reshape.151 = bf16[16,8,3,8,64]{4,3,2,1,0:T(8,128)(2,1)S(1)} reshape(bf16[128,1536]{1,0:T(8,128)(2,1)S(1)} %convolution_convert_fusion) | data formatting | bytes 786432 | tf_op jit(solution)/shard_map/reshape | solution.py:57
  25.5 0.9 %fusion.66 = (bf16[16,8,1,8,64]{4,3,2,1,0:T(8,128)(2,1)S(1)}, bf16[16,8,1,8,64]{4,3,2,1,0:T(8,128)(2,1)}, bf16[16,8,1,8,64]{4,3,2,1,0:T(8,128)(2,1)S(1)}) fusion(bf16[16,8,3,8,64]{4,3,2,1,0:T(8,128)(2,1)S(1)} %reshape.151), kind=kLoop, calls=%fused_computation.88 | loop fusion | bytes 786432 | tf_op jit(solution)/shard_map/slice | solution.py:59
  26.5 1.1 %fusion.68 = f32[8,8,16]{2,1,0:T(8,128)} fusion(bf16[16,8,1,8,64]{4,3,2,1,0:T(8,128)(2,1)S(1)} %get-tuple-element.40, bf16[16,8,1,8,64]{4,3,2,1,0:T(8,128)(2,1)S(1)} %get-tuple-element.33), kind=kOutput, calls=%fused_computation.90 | convolution fusion | flops 2146319 | bytes 266240 | tf_op jit(solution)/shard_map/sub | solution.py:17
  27.6 0.4 convolution_multiply_fusion.1
  28.0 0.0 copy-start.3
  28.0 1.4 %fusion.6 = bf16[16,8,8,64]{3,0,2,1:T(8,128)(2,1)S(1)} fusion(bf16[16,8,1,8,64]{4,3,2,1,0:T(8,128)(2,1)} %get-tuple-element.34, f32[8,8,16]{2,1,0:T(8,128)} %fusion.68, f32[8,8,16,16]{2,3,1,0:T(8,128)S(1)} %convolution_multiply_fusion.1), kind=kOutput, calls=%fused_computation.12 | convolution fusion | flops 2212879 | bytes 331776 | tf_op jit(solution)/shard_map/khfg,gkhd->fkhd/dot_general | solution.py:62
  29.4 0.1 copy.30
  29.5 0.2 reshape.152
  29.7 0.0 copy-done.3
  29.7 0.2 fusion.11
  30.0 10.5 %all_to_all.9 = bf16[16,1,8,512]{3,2,1,0:T(8,128)(2,1)S(1)} all-to-all(bf16[16,1,8,512]{3,2,1,0:T(8,128)(2,1)S(1)} %fusion.11), channel_id=1, replica_groups=mesh['groups'=2,'seq'=16] {'seq'}, dimensions={0} | all-to-all | bytes 262144 | tf_op jit(solution)/shard_map/all_to_all | solution.py:96
  40.5 0.1 convert_reduce_fusion
  40.6 0.1 div.58
  40.7 0.2 fusion.40
  40.9 0.1 rsqrt.35
  41.0 0.0 copy-done
  41.0 3.2 %fusion.10 = bf16[1,128,512]{2,1,0:T(8,128)(2,1)} fusion(bf16[2048,512]{1,0:T(8,128)(2,1)S(1)} %copy-done, bf16[16,1,8,512]{3,2,1,0:T(8,128)(2,1)S(1)} %all_to_all.9, bf16[512,2048]{1,0:T(8,128)(2,1)} %param.12, f32[128]{0:T(128)S(1)} %rsqrt.35, f32[128]{0:T(128)S(1)} %div.58), kind=kOutput, calls=%fused_computation.20 | convolution fusion | flops 539688960 | bytes 4457472 | tf_op jit(solution)/shard_map/dot_general | solution.py:77
  (6 shorter events, 0.0 us)
Async XLA Ops:
  0.0 41.0 %copy-start = (bf16[2048,512]{1,0:T(8,128)(2,1)S(1)}, bf16[2048,512]{1,0:T(8,128)(2,1)}, u32[]{:S(2)}) copy-start(bf16[2048,512]{1,0:T(8,128)(2,1)} %param.13) | copy-start | bytes 6291460
  4.4 3.0 %copy-start.1 = (bf16[1,128,512]{2,1,0:T(8,128)(2,1)S(1)}, bf16[1,128,512]{2,1,0:T(8,128)(2,1)}, u32[]{:S(2)}) copy-start(bf16[1,128,512]{2,1,0:T(8,128)(2,1)} %param.7) | copy-start | bytes 393220
  4.4 3.0 %copy-start.2 = (bf16[512,512]{1,0:T(8,128)(2,1)S(1)}, bf16[512,512]{1,0:T(8,128)(2,1)}, u32[]{:S(2)}) copy-start(bf16[512,512]{1,0:T(8,128)(2,1)} %param.9) | copy-start | bytes 1572868
  28.0 1.7 %copy-start.3 = (bf16[512,512]{1,0:T(8,128)(2,1)S(1)}, bf16[512,512]{1,0:T(8,128)(2,1)}, u32[]{:S(2)}) copy-start(bf16[512,512]{1,0:T(8,128)(2,1)} %param.11) | copy-start | bytes 1572868
where the time goes:
time: 44.5 us; the launch traced here: 44.1 us
  blocking collectives  25.6 us (58%)
  matrix products  13.3 us (30%)
  other arithmetic  2.81 us (6%)
  local copies, waits for them, and re-layouts  2.23 us (5%)
    all_to_all x1, blocking collectives, local(): lax.all_to_all(blocks, 'seq', split_axis=1, concat_axis=0, tiled=True)  15.1 us
    all_to_all x1, blocking collectives, local(): lax.all_to_all(returned, 'seq', split_axis=0, concat_axis=1, tiled=True)  10.5 us
    dot_general x1, matrix products, feed_forward(): jnp.dot(hidden, w_down, preferred_element_type=jnp.float32)  3.19 us
    dot_general x1, matrix products, spatial_frame(): jnp.dot(norm_rows(frame_rows.astype(jnp.float32)), w_qkv, preferred_eleme...  1.9 us
    dot_general x1, matrix products, temporal_block(): jnp.dot(norm_rows(flat_rows.astype(jnp.float32)), w_qkv, preferred_elemen...  1.82 us
    sub x2, matrix products, softmax_rows(): raised = jnp.exp(scores - row_max)  1.51 us
    dot_general x1, matrix products, one_block(): jnp.einsum('hqk,khd->qhd', weights, value_rows, preferred_element_type=jn...  1.47 us
    reduce_sum x3, other arithmetic, norm_rows(): spread = jnp.mean(center * center, axis=-1, keepdims=True)  1.43 us

commit v1 on v0

--- a/solution.py
+++ b/solution.py
@@ -93,7 +93,20 @@
     tokens = arrived.reshape(frames, count_rows, model_width)
     after_time = temporal_block(tokens, temporal_qkv, temporal_out)
     returned = after_time.reshape(frames, 1, count_rows, model_width)
-    arrived_back = lax.all_to_all(returned, "seq", split_axis=0, concat_axis=1, tiled=True)
+    ways, here = (lax.axis_size("seq"), lax.axis_index("seq"))
+    width = returned.shape[0] // ways
+    dims = list(returned.shape)
+    dims[0] = width
+    height = dims[1]
+    dims[1] = height * ways
+    arrived_back = jnp.zeros(dims, returned.dtype)
+    for mask in range(ways):
+        part = lax.dynamic_slice_in_dim(returned, (here ^ mask) * width, width, axis=0)
+        if mask:
+            part = lax.ppermute(part, "seq", [(d, d ^ mask) for d in range(ways)])
+        arrived_back = lax.dynamic_update_slice_in_dim(
+            arrived_back, part, (here ^ mask) * height, axis=1
+        )
     result_rows = arrived_back.reshape(frame_count * patches, model_width)
     result_rows = feed_forward(result_rows, mlp_up, mlp_down)
     return result_rows.reshape(frame_count, patches, model_width)

time: 44.5 us -> 58 us (1.30)
  starting transfers between devices: 0 us -> 28 us
  blocking collectives: 25.6 us -> 0 us
  waiting for transfers between devices: 0 us -> 10.2 us
  matrix products: 13.3 us -> 13.9 us
    all_to_all x2 -> x0, blocking collectives: 25.6 us -> none  [the longest x1 15.1 us: local(): lax.all_to_all(blocks, 'seq', split_axis=1, concat_axis=0, tiled=True)]
    ppermute x0 -> x15, starting transfers between devices: none -> 20.5 us  [local(): part = lax.ppermute(part, 'seq', [(d, d ^ mask) for d in range(ways)])]
    all_to_all x0 -> x1, waiting for transfers between devices: none -> 7.82 us  [local(): lax.all_to_all(blocks, 'seq', split_axis=1, concat_axis=0, tiled=True)]
    all_to_all x0 -> x1, starting transfers between devices: none -> 7.41 us  [local(): lax.all_to_all(blocks, 'seq', split_axis=1, concat_axis=0, tiled=True)]
    ppermute x0 -> x15, waiting for transfers between devices: none -> 2.38 us  [local(): part = lax.ppermute(part, 'seq', [(d, d ^ mask) for d in range(ways)])]
    dot_general x1, matrix products: 0.25 us -> 0.91 us  [spatial_frame(): jnp.dot(attended, w_out, preferred_element_type=jnp.float32)]
  transfers between devices with their start and end apart: 0 -> 16, of which waited for: 0 -> 3; matrix products, arithmetic and copies ran while one was open for 0% -> 0% of each run, Pallas kernels for 0% -> 0%
where the time goes in v1:
time: 58 us; the launch traced here: 57.7 us
  starting transfers between devices  28 us (48%)
  matrix products  13.9 us (24%)
  waiting for transfers between devices  10.2 us (18%)
  other arithmetic  2.81 us (5%)
  local copies, waits for them, and re-layouts  2.37 us (4%)
    ppermute x15, starting transfers between devices, local(): part = lax.ppermute(part, 'seq', [(d, d ^ mask) for d in range(ways)])  20.5 us
    all_to_all x1, waiting for transfers between devices, local(): lax.all_to_all(blocks, 'seq', split_axis=1, concat_axis=0, tiled=True)  7.82 us
    all_to_all x1, starting transfers between devices, local(): lax.all_to_all(blocks, 'seq', split_axis=1, concat_axis=0, tiled=True)  7.41 us
    dot_general x1, matrix products, feed_forward(): jnp.dot(hidden, w_down, preferred_element_type=jnp.float32)  3.19 us
    ppermute x15, waiting for transfers between devices, local(): part = lax.ppermute(part, 'seq', [(d, d ^ mask) for d in range(ways)])  2.38 us
    dot_general x1, matrix products, spatial_frame(): jnp.dot(norm_rows(frame_rows.astype(jnp.float32)), w_qkv, preferred_eleme...  1.9 us
    dot_general x1, matrix products, temporal_block(): jnp.dot(norm_rows(flat_rows.astype(jnp.float32)), w_qkv, preferred_elemen...  1.83 us
    sub x2, matrix products, softmax_rows(): raised = jnp.exp(scores - row_max)  1.52 us
  transfers between devices with their start and end apart: 16, of which 3 were waited for; matrix products, arithmetic and copies ran while one was open for 0% of the time, Pallas kernels for 0%

profile of v1, /device:TPU:0, one launch (start us, length us, event | category | flops | bytes accessed | tf_op | source)
XLA Modules:
  0.0 57.7 jit_solution(13901902067970848285)
XLA Ops:
  0.0 0.0 copy-start
  0.0 1.2 %convert_reduce_fusion.2 = f32[128]{0:T(128)S(1)} fusion(bf16[1,128,512]{2,1,0:T(8,128)(2,1)} %param.7), kind=kLoop, calls=%fused_computation.45 | loop fusion | flops 130944 | bytes 131584 | tf_op jit(solution)/shard_map/while/body/eval_jaxpr/reduce_sum | solution.py:10
  1.2 1.1 %fusion.31 = f32[128]{0:T(128)S(1)} fusion(bf16[1,128,512]{2,1,0:T(8,128)(2,1)} %param.7, f32[128]{0:T(128)S(1)} %broadcast_multiply_fusion.2), kind=kLoop, calls=%fused_computation.50 | loop fusion | flops 262016 | bytes 132096 | tf_op jit(solution)/shard_map/while/body/eval_jaxpr/reduce_sum | solution.py:11
  2.3 1.9 %convolution_convert_fusion.1 = bf16[128,1536]{1,0:T(8,128)(2,1)S(1)} fusion(bf16[512,1536]{1,0:T(8,128)(2,1)} %param.8, bf16[1,128,512]{2,1,0:T(8,128)(2,1)} %param.7, f32[128]{0:T(128)S(1)} %add_rsqrt_fusion.2, f32[128]{0:T(128)S(1)} %broadcast_multiply_fusion.2), kind=kOutput, calls=%fused_computation.3 | convolution fusion | flops 201785344 | bytes 2098176 | tf_op jit(solution)/shard_map/while/body/eval_jaxpr/dot_general | solution.py:24
  4.2 0.2 copy.55
  4.4 0.0 copy-start.1
  4.4 0.0 copy-start.2
  4.4 1.1 %convolution_multiply_fusion = f32[8,128,128]{1,2,0:T(8,128)} fusion(bf16[128,3,8,64]{0,3,2,1:T(8,128)(2,1)S(1)} %bitcast.133), kind=kOutput, calls=%fused_computation.9 | convolution fusion | flops 16908288 | bytes 786432 | tf_op jit(solution)/shard_map/while/body/eval_jaxpr/while/body/eval_jaxpr/qhd,khd->hqk/dot_general | solution.py:34
  5.5 0.4 fusion.67
  5.9 1.5 %convolution_convert_fusion.3 = bf16[8,64,128]{2,1,0:T(8,128)(2,1)S(1)} fusion(f32[8,128]{1,0:T(8,128)S(1)} %fusion.67, bf16[128,3,8,64]{0,3,2,1:T(8,128)(2,1)S(1)} %bitcast.135, f32[8,128,128]{1,2,0:T(8,128)} %convolution_multiply_fusion), kind=kOutput, calls=%fused_computation.19 | convolution fusion | flops 17237120 | bytes 1314816 | tf_op jit(solution)/shard_map/while/body/eval_jaxpr/while/body/eval_jaxpr/hqk,khd->qhd/dot_general | solution.py:38
  7.4 0.0 copy-done.1
  7.4 0.0 copy-done.2
  7.4 0.9 %fusion.12 = bf16[1,16,8,512]{3,2,0,1:T(8,128)(2,1)} fusion(bf16[128,512]{0,1:T(8,128)(2,1)S(1)} %bitcast.136, bf16[512,512]{1,0:T(8,128)(2,1)S(1)} %copy-done.2, bf16[1,128,512]{2,1,0:T(8,128)(2,1)S(1)} %copy-done.1), kind=kOutput, calls=%fused_computation.22 | convolution fusion | flops 67305472 | bytes 917504 | tf_op jit(solution)/shard_map/while/body/eval_jaxpr/dot_general | solution.py:44
  8.3 7.4 %all-to-all-start = ((bf16[1,16,8,512]{3,2,0,1:T(8,128)(2,1)}), bf16[1,16,8,512]{3,2,0,1:T(8,128)(2,1)S(1)}, u32[]{:S(2)}, u32[]{:S(2)}) async-start(bf16[1,16,8,512]{3,2,0,1:T(8,128)(2,1)} %fusion.12), calls=%async_computation | async-start | bytes 262144 | tf_op jit(solution)/shard_map/all_to_all | solution.py:90
  15.8 7.8 %all-to-all-done = bf16[1,16,8,512]{3,2,0,1:T(8,128)(2,1)S(1)} async-done(((bf16[1,16,8,512]{3,2,0,1:T(8,128)(2,1)}), bf16[1,16,8,512]{3,2,0,1:T(8,128)(2,1)S(1)}, u32[]{:S(2)}, u32[]{:S(2)}) %all-to-all-start) | async-done | bytes 131104 | tf_op jit(solution)/shard_map/all_to_all | solution.py:90
  23.6 0.1 convert_reduce_fusion.1
  23.7 0.1 div.53
  23.8 0.2 fusion.38
  24.0 0.1 rsqrt.33
  24.1 1.8 %convolution_convert_fusion = bf16[128,1536]{1,0:T(8,128)(2,1)S(1)} fusion(bf16[512,1536]{1,0:T(8,128)(2,1)} %param.10, bf16[1,16,8,512]{3,2,0,1:T(8,128)(2,1)S(1)} %all-to-all-done, f32[128]{0:T(128)S(1)} %rsqrt.33, f32[128]{0:T(128)S(1)} %div.53), kind=kOutput, calls=%fused_computation.2 | convolution fusion | flops 201785344 | bytes 2098176 | tf_op jit(solution)/shard_map/dot_general | solution.py:54
  25.9 0.4 reshape.137
  26.4 0.9 %fusion.66 = (bf16[16,8,1,8,64]{4,3,2,1,0:T(8,128)(2,1)S(1)}, bf16[16,8,1,8,64]{4,3,2,1,0:T(8,128)(2,1)}, bf16[16,8,1,8,64]{4,3,2,1,0:T(8,128)(2,1)S(1)}) fusion(bf16[16,8,3,8,64]{4,3,2,1,0:T(8,128)(2,1)S(1)} %reshape.137), kind=kLoop, calls=%fused_computation.119 | loop fusion | bytes 786432 | tf_op jit(solution)/shard_map/slice | solution.py:59
  27.3 0.4 convolution_multiply_fusion.1
  27.7 1.2 %fusion.68 = f32[8,8,16]{2,1,0:T(8,128)} fusion(bf16[16,8,1,8,64]{4,3,2,1,0:T(8,128)(2,1)S(1)} %get-tuple-element.40, bf16[16,8,1,8,64]{4,3,2,1,0:T(8,128)(2,1)S(1)} %get-tuple-element.33), kind=kOutput, calls=%fused_computation.121 | convolution fusion | flops 2146319 | bytes 266240 | tf_op jit(solution)/shard_map/sub | solution.py:17
  28.9 1.4 %fusion.6 = bf16[16,8,8,64]{3,0,2,1:T(8,128)(2,1)S(1)} fusion(bf16[16,8,1,8,64]{4,3,2,1,0:T(8,128)(2,1)} %get-tuple-element.34, f32[8,8,16]{2,1,0:T(8,128)} %fusion.68, f32[8,8,16,16]{2,3,1,0:T(8,128)S(1)} %convolution_multiply_fusion.1), kind=kOutput, calls=%fused_computation.12 | convolution fusion | flops 2212879 | bytes 331776 | tf_op jit(solution)/shard_map/khfg,gkhd->fkhd/dot_general | solution.py:62
  30.3 0.1 copy.62
  30.4 0.2 reshape.138
  30.6 0.2 fusion.11
  30.8 0.1 constant_dynamic-slice_fusion
  30.9 0.1 collective-permute-start
  31.0 0.1 collective-permute-start.1
  31.1 1.8 %collective-permute-start.2 = (bf16[1,1,8,512]{3,2,0,1:T(8,128)(2,1)S(1)}, bf16[1,1,8,512]{3,2,0,1:T(8,128)(2,1)S(1)}, u32[]{:S(2)}, u32[]{:S(2)}) collective-permute-start(bf16[1,1,8,512]{3,2,0,1:T(8,128)(2,1)S(1)} %get-tuple-element.55), channel_id=1, source_target_pairs={{0,3},{1,2},{2,1},{3,0},{4,7},{5,6},{6,5},{7,4},{8,11},{9,10},{10,... | collective-permute-start | bytes 24584 | tf_op jit(solution)/shard_map/ppermute | solution.py:106
  32.8 0.0 collective-permute-start.3
  32.9 1.7 %collective-permute-start.4 = (bf16[1,1,8,512]{3,2,0,1:T(8,128)(2,1)S(1)}, bf16[1,1,8,512]{3,2,0,1:T(8,128)(2,1)S(1)}, u32[]{:S(2)}, u32[]{:S(2)}) collective-permute-start(bf16[1,1,8,512]{3,2,0,1:T(8,128)(2,1)S(1)} %get-tuple-element.53), channel_id=1, source_target_pairs={{0,5},{1,4},{2,7},{3,6},{4,1},{5,0},{6,3},{7,2},{8,13},{9,12},{10,... | collective-permute-start | bytes 24584 | tf_op jit(solution)/shard_map/ppermute | solution.py:106
  34.6 0.0 collective-permute-done
  34.6 0.2 collective-permute-start.5
  34.8 0.0 collective-permute-done.1
  34.8 2.6 %collective-permute-start.6 = (bf16[1,1,8,512]{3,2,0,1:T(8,128)(2,1)S(1)}, bf16[1,1,8,512]{3,2,0,1:T(8,128)(2,1)S(1)}, u32[]{:S(2)}, u32[]{:S(2)}) collective-permute-start(bf16[1,1,8,512]{3,2,0,1:T(8,128)(2,1)S(1)} %get-tuple-element.51), channel_id=1, source_target_pairs={{0,7},{1,6},{2,5},{3,4},{4,3},{5,2},{6,1},{7,0},{8,15},{9,14},{10,... | collective-permute-start | bytes 24584 | tf_op jit(solution)/shard_map/ppermute | solution.py:106
  37.4 0.0 collective-permute-done.2
  37.4 0.4 collective-permute-start.7
  37.8 0.0 collective-permute-done.3
  37.8 2.2 %collective-permute-start.8 = (bf16[1,1,8,512]{3,2,0,1:T(8,128)(2,1)S(1)}, bf16[1,1,8,512]{3,2,0,1:T(8,128)(2,1)S(1)}, u32[]{:S(2)}, u32[]{:S(2)}) collective-permute-start(bf16[1,1,8,512]{3,2,0,1:T(8,128)(2,1)S(1)} %get-tuple-element.49), channel_id=1, source_target_pairs={{0,9},{1,8},{2,11},{3,10},{4,13},{5,12},{6,15},{7,14},{8,1},{9,0},... | collective-permute-start | bytes 24584 | tf_op jit(solution)/shard_map/ppermute | solution.py:106
  40.0 0.0 collective-permute-done.4
  40.0 0.3 collective-permute-start.9
  40.3 0.0 collective-permute-done.5
  40.3 3.3 %collective-permute-start.10 = (bf16[1,1,8,512]{3,2,0,1:T(8,128)(2,1)S(1)}, bf16[1,1,8,512]{3,2,0,1:T(8,128)(2,1)S(1)}, u32[]{:S(2)}, u32[]{:S(2)}) collective-permute-start(bf16[1,1,8,512]{3,2,0,1:T(8,128)(2,1)S(1)} %get-tuple-element.47), channel_id=1, source_target_pairs={{0,11},{1,10},{2,9},{3,8},{4,15},{5,14},{6,13},{7,12},{8,3},{9,2},... | collective-permute-start | bytes 24584 | tf_op jit(solution)/shard_map/ppermute | solution.py:106
  43.6 0.0 collective-permute-done.6
  43.6 0.7 %collective-permute-start.11 = (bf16[1,1,8,512]{3,2,0,1:T(8,128)(2,1)S(1)}, bf16[1,1,8,512]{3,2,0,1:T(8,128)(2,1)S(1)}, u32[]{:S(2)}, u32[]{:S(2)}) collective-permute-start(bf16[1,1,8,512]{3,2,0,1:T(8,128)(2,1)S(1)} %get-tuple-element.46), channel_id=1, source_target_pairs={{0,12},{1,13},{2,14},{3,15},{4,8},{5,9},{6,10},{7,11},{8,4},{9,5},... | collective-permute-start | bytes 24584 | tf_op jit(solution)/shard_map/ppermute | solution.py:106
  44.3 0.0 collective-permute-done.7
  44.3 2.8 %collective-permute-start.12 = (bf16[1,1,8,512]{3,2,0,1:T(8,128)(2,1)S(1)}, bf16[1,1,8,512]{3,2,0,1:T(8,128)(2,1)S(1)}, u32[]{:S(2)}, u32[]{:S(2)}) collective-permute-start(bf16[1,1,8,512]{3,2,0,1:T(8,128)(2,1)S(1)} %get-tuple-element.45), channel_id=1, source_target_pairs={{0,13},{1,12},{2,15},{3,14},{4,9},{5,8},{6,11},{7,10},{8,5},{9,4},... | collective-permute-start | bytes 24584 | tf_op jit(solution)/shard_map/ppermute | solution.py:106
  47.1 0.0 collective-permute-done.8
  47.1 1.1 %collective-permute-start.13 = (bf16[1,1,8,512]{3,2,0,1:T(8,128)(2,1)S(1)}, bf16[1,1,8,512]{3,2,0,1:T(8,128)(2,1)S(1)}, u32[]{:S(2)}, u32[]{:S(2)}) collective-permute-start(bf16[1,1,8,512]{3,2,0,1:T(8,128)(2,1)S(1)} %get-tuple-element.44), channel_id=1, source_target_pairs={{0,14},{1,15},{2,12},{3,13},{4,10},{5,11},{6,8},{7,9},{8,6},{9,7},... | collective-permute-start | bytes 24584 | tf_op jit(solution)/shard_map/ppermute | solution.py:106
  48.2 0.0 collective-permute-done.9
  48.2 3.4 %collective-permute-start.14 = (bf16[1,1,8,512]{3,2,0,1:T(8,128)(2,1)S(1)}, bf16[1,1,8,512]{3,2,0,1:T(8,128)(2,1)S(1)}, u32[]{:S(2)}, u32[]{:S(2)}) collective-permute-start(bf16[1,1,8,512]{3,2,0,1:T(8,128)(2,1)S(1)} %get-tuple-element.42), channel_id=1, source_target_pairs={{0,15},{1,14},{2,13},{3,12},{4,11},{5,10},{6,9},{7,8},{8,7},{9,6},... | collective-permute-start | bytes 24584 | tf_op jit(solution)/shard_map/ppermute | solution.py:106
  51.6 0.0 collective-permute-done.10
  51.6 0.0 collective-permute-done.11
  51.6 0.0 collective-permute-done.12
  51.6 1.8 %collective-permute-done.13 = bf16[1,1,8,512]{3,2,0,1:T(8,128)(2,1)S(1)} collective-permute-done((bf16[1,1,8,512]{3,2,0,1:T(8,128)(2,1)S(1)}, bf16[1,1,8,512]{3,2,0,1:T(8,128)(2,1)S(1)}, u32[]{:S(2)}, u32[]{:S(2)}) %collective-permute-start.13) | collective-permute-done | bytes 8224 | tf_op jit(solution)/shard_map/ppermute | solution.py:106
  53.4 0.5 collective-permute-done.14
  54.0 0.1 convert_reduce_fusion
  54.1 0.2 fusion.40
  54.3 0.1 div.58
  54.4 0.1 rsqrt.35
  54.5 3.2 %fusion.10 = bf16[1,128,512]{2,1,0:T(8,128)(2,1)} fusion(bf16[2048,512]{1,0:T(8,128)(2,1)S(1)} %copy-done, bf16[1,16,8,512]{3,2,1,0:T(8,128)(2,1)S(1)} %bitcast_dynamic-update-slice_fusion, bf16[512,2048]{1,0:T(8,128)(2,1)} %param.12, f32[128]{0:T(128)S(1)} %rsqrt.35, f32[128]{0:T(128)S(1)} %div.58), kind=kOutput, calls=%fused_computation.20 | convolution fusion | flops 539688960 | bytes 4457472 | tf_op jit(solution)/shard_map/dot_general | solution.py:77
  (26 shorter events, 0.1 us)
Async XLA Ops:
  0.0 54.5 %copy-start = (bf16[2048,512]{1,0:T(8,128)(2,1)S(1)}, bf16[2048,512]{1,0:T(8,128)(2,1)}, u32[]{:S(2)}) copy-start(bf16[2048,512]{1,0:T(8,128)(2,1)} %param.13) | copy-start | bytes 6291460
  4.4 3.0 %copy-start.1 = (bf16[1,128,512]{2,1,0:T(8,128)(2,1)S(1)}, bf16[1,128,512]{2,1,0:T(8,128)(2,1)}, u32[]{:S(2)}) copy-start(bf16[1,128,512]{2,1,0:T(8,128)(2,1)} %param.7) | copy-start | bytes 393220
  4.4 3.0 %copy-start.2 = (bf16[512,512]{1,0:T(8,128)(2,1)S(1)}, bf16[512,512]{1,0:T(8,128)(2,1)}, u32[]{:S(2)}) copy-start(bf16[512,512]{1,0:T(8,128)(2,1)} %param.9) | copy-start | bytes 1572868
  8.3 15.3 %all-to-all-start = ((bf16[1,16,8,512]{3,2,0,1:T(8,128)(2,1)}), bf16[1,16,8,512]{3,2,0,1:T(8,128)(2,1)S(1)}, u32[]{:S(2)}, u32[]{:S(2)}) async-start(bf16[1,16,8,512]{3,2,0,1:T(8,128)(2,1)} %fusion.12), calls=%async_computation | async-start | bytes 262144 | tf_op jit(solution)/shard_map/all_to_all | solution.py:90
  28.9 1.7 %copy-start.3 = (bf16[512,512]{1,0:T(8,128)(2,1)S(1)}, bf16[512,512]{1,0:T(8,128)(2,1)}, u32[]{:S(2)}) copy-start(bf16[512,512]{1,0:T(8,128)(2,1)} %param.11) | copy-start | bytes 1572868
  30.9 3.7 %collective-permute-start = (bf16[1,1,8,512]{3,2,0,1:T(8,128)(2,1)S(1)}, bf16[1,1,8,512]{3,2,0,1:T(8,128)(2,1)S(1)}, u32[]{:S(2)}, u32[]{:S(2)}) collective-permute-start(bf16[1,1,8,512]{3,2,0,1:T(8,128)(2,1)S(1)} %get-tuple-element.57), channel_id=1, source_target_pairs={{0,1},{1,0},{2,3},{3,2},{4,5},{5,4},{6,7},{7,6},{8,9},{9,8},{10,11... | collective-permute-start | bytes 24584 | tf_op jit(solution)/shard_map/ppermute | solution.py:106
  31.0 3.8 %collective-permute-start.1 = (bf16[1,1,8,512]{3,2,0,1:T(8,128)(2,1)S(1)}, bf16[1,1,8,512]{3,2,0,1:T(8,128)(2,1)S(1)}, u32[]{:S(2)}, u32[]{:S(2)}) collective-permute-start(bf16[1,1,8,512]{3,2,0,1:T(8,128)(2,1)S(1)} %get-tuple-element.56), channel_id=1, source_target_pairs={{0,2},{1,3},{2,0},{3,1},{4,6},{5,7},{6,4},{7,5},{8,10},{9,11},{10,... | collective-permute-start | bytes 24584 | tf_op jit(solution)/shard_map/ppermute | solution.py:106
  31.1 6.3 %collective-permute-start.2 = (bf16[1,1,8,512]{3,2,0,1:T(8,128)(2,1)S(1)}, bf16[1,1,8,512]{3,2,0,1:T(8,128)(2,1)S(1)}, u32[]{:S(2)}, u32[]{:S(2)}) collective-permute-start(bf16[1,1,8,512]{3,2,0,1:T(8,128)(2,1)S(1)} %get-tuple-element.55), channel_id=1, source_target_pairs={{0,3},{1,2},{2,1},{3,0},{4,7},{5,6},{6,5},{7,4},{8,11},{9,10},{10,... | collective-permute-start | bytes 24584 | tf_op jit(solution)/shard_map/ppermute | solution.py:106
  32.8 4.9 %collective-permute-start.3 = (bf16[1,1,8,512]{3,2,0,1:T(8,128)(2,1)S(1)}, bf16[1,1,8,512]{3,2,0,1:T(8,128)(2,1)S(1)}, u32[]{:S(2)}, u32[]{:S(2)}) collective-permute-start(bf16[1,1,8,512]{3,2,0,1:T(8,128)(2,1)S(1)} %get-tuple-element.54), channel_id=1, source_target_pairs={{0,4},{1,5},{2,6},{3,7},{4,0},{5,1},{6,2},{7,3},{8,12},{9,13},{10,... | collective-permute-start | bytes 24584 | tf_op jit(solution)/shard_map/ppermute | solution.py:106
  32.9 7.1 %collective-permute-start.4 = (bf16[1,1,8,512]{3,2,0,1:T(8,128)(2,1)S(1)}, bf16[1,1,8,512]{3,2,0,1:T(8,128)(2,1)S(1)}, u32[]{:S(2)}, u32[]{:S(2)}) collective-permute-start(bf16[1,1,8,512]{3,2,0,1:T(8,128)(2,1)S(1)} %get-tuple-element.53), channel_id=1, source_target_pairs={{0,5},{1,4},{2,7},{3,6},{4,1},{5,0},{6,3},{7,2},{8,13},{9,12},{10,... | collective-permute-start | bytes 24584 | tf_op jit(solution)/shard_map/ppermute | solution.py:106
  34.6 5.7 %collective-permute-start.5 = (bf16[1,1,8,512]{3,2,0,1:T(8,128)(2,1)S(1)}, bf16[1,1,8,512]{3,2,0,1:T(8,128)(2,1)S(1)}, u32[]{:S(2)}, u32[]{:S(2)}) collective-permute-start(bf16[1,1,8,512]{3,2,0,1:T(8,128)(2,1)S(1)} %get-tuple-element.52), channel_id=1, source_target_pairs={{0,6},{1,7},{2,4},{3,5},{4,2},{5,3},{6,0},{7,1},{8,14},{9,15},{10,... | collective-permute-start | bytes 24584 | tf_op jit(solution)/shard_map/ppermute | solution.py:106
  34.8 8.8 %collective-permute-start.6 = (bf16[1,1,8,512]{3,2,0,1:T(8,128)(2,1)S(1)}, bf16[1,1,8,512]{3,2,0,1:T(8,128)(2,1)S(1)}, u32[]{:S(2)}, u32[]{:S(2)}) collective-permute-start(bf16[1,1,8,512]{3,2,0,1:T(8,128)(2,1)S(1)} %get-tuple-element.51), channel_id=1, source_target_pairs={{0,7},{1,6},{2,5},{3,4},{4,3},{5,2},{6,1},{7,0},{8,15},{9,14},{10,... | collective-permute-start | bytes 24584 | tf_op jit(solution)/shard_map/ppermute | solution.py:106
  37.4 6.9 %collective-permute-start.7 = (bf16[1,1,8,512]{3,2,0,1:T(8,128)(2,1)S(1)}, bf16[1,1,8,512]{3,2,0,1:T(8,128)(2,1)S(1)}, u32[]{:S(2)}, u32[]{:S(2)}) collective-permute-start(bf16[1,1,8,512]{3,2,0,1:T(8,128)(2,1)S(1)} %get-tuple-element.50), channel_id=1, source_target_pairs={{0,8},{1,9},{2,10},{3,11},{4,12},{5,13},{6,14},{7,15},{8,0},{9,1},... | collective-permute-start | bytes 24584 | tf_op jit(solution)/shard_map/ppermute | solution.py:106
  37.8 9.3 %collective-permute-start.8 = (bf16[1,1,8,512]{3,2,0,1:T(8,128)(2,1)S(1)}, bf16[1,1,8,512]{3,2,0,1:T(8,128)(2,1)S(1)}, u32[]{:S(2)}, u32[]{:S(2)}) collective-permute-start(bf16[1,1,8,512]{3,2,0,1:T(8,128)(2,1)S(1)} %get-tuple-element.49), channel_id=1, source_target_pairs={{0,9},{1,8},{2,11},{3,10},{4,13},{5,12},{6,15},{7,14},{8,1},{9,0},... | collective-permute-start | bytes 24584 | tf_op jit(solution)/shard_map/ppermute | solution.py:106
  40.0 8.2 %collective-permute-start.9 = (bf16[1,1,8,512]{3,2,0,1:T(8,128)(2,1)S(1)}, bf16[1,1,8,512]{3,2,0,1:T(8,128)(2,1)S(1)}, u32[]{:S(2)}, u32[]{:S(2)}) collective-permute-start(bf16[1,1,8,512]{3,2,0,1:T(8,128)(2,1)S(1)} %get-tuple-element.48), channel_id=1, source_target_pairs={{0,10},{1,11},{2,8},{3,9},{4,14},{5,15},{6,12},{7,13},{8,2},{9,3},... | collective-permute-start | bytes 24584 | tf_op jit(solution)/shard_map/ppermute | solution.py:106
  40.3 11.3 %collective-permute-start.10 = (bf16[1,1,8,512]{3,2,0,1:T(8,128)(2,1)S(1)}, bf16[1,1,8,512]{3,2,0,1:T(8,128)(2,1)S(1)}, u32[]{:S(2)}, u32[]{:S(2)}) collective-permute-start(bf16[1,1,8,512]{3,2,0,1:T(8,128)(2,1)S(1)} %get-tuple-element.47), channel_id=1, source_target_pairs={{0,11},{1,10},{2,9},{3,8},{4,15},{5,14},{6,13},{7,12},{8,3},{9,2},... | collective-permute-start | bytes 24584 | tf_op jit(solution)/shard_map/ppermute | solution.py:106
  43.6 8.0 %collective-permute-start.11 = (bf16[1,1,8,512]{3,2,0,1:T(8,128)(2,1)S(1)}, bf16[1,1,8,512]{3,2,0,1:T(8,128)(2,1)S(1)}, u32[]{:S(2)}, u32[]{:S(2)}) collective-permute-start(bf16[1,1,8,512]{3,2,0,1:T(8,128)(2,1)S(1)} %get-tuple-element.46), channel_id=1, source_target_pairs={{0,12},{1,13},{2,14},{3,15},{4,8},{5,9},{6,10},{7,11},{8,4},{9,5},... | collective-permute-start | bytes 24584 | tf_op jit(solution)/shard_map/ppermute | solution.py:106
  44.3 7.4 %collective-permute-start.12 = (bf16[1,1,8,512]{3,2,0,1:T(8,128)(2,1)S(1)}, bf16[1,1,8,512]{3,2,0,1:T(8,128)(2,1)S(1)}, u32[]{:S(2)}, u32[]{:S(2)}) collective-permute-start(bf16[1,1,8,512]{3,2,0,1:T(8,128)(2,1)S(1)} %get-tuple-element.45), channel_id=1, source_target_pairs={{0,13},{1,12},{2,15},{3,14},{4,9},{5,8},{6,11},{7,10},{8,5},{9,4},... | collective-permute-start | bytes 24584 | tf_op jit(solution)/shard_map/ppermute | solution.py:106
  47.1 6.3 %collective-permute-start.13 = (bf16[1,1,8,512]{3,2,0,1:T(8,128)(2,1)S(1)}, bf16[1,1,8,512]{3,2,0,1:T(8,128)(2,1)S(1)}, u32[]{:S(2)}, u32[]{:S(2)}) collective-permute-start(bf16[1,1,8,512]{3,2,0,1:T(8,128)(2,1)S(1)} %get-tuple-element.44), channel_id=1, source_target_pairs={{0,14},{1,15},{2,12},{3,13},{4,10},{5,11},{6,8},{7,9},{8,6},{9,7},... | collective-permute-start | bytes 24584 | tf_op jit(solution)/shard_map/ppermute | solution.py:106
  48.2 5.8 %collective-permute-start.14 = (bf16[1,1,8,512]{3,2,0,1:T(8,128)(2,1)S(1)}, bf16[1,1,8,512]{3,2,0,1:T(8,128)(2,1)S(1)}, u32[]{:S(2)}, u32[]{:S(2)}) collective-permute-start(bf16[1,1,8,512]{3,2,0,1:T(8,128)(2,1)S(1)} %get-tuple-element.42), channel_id=1, source_target_pairs={{0,15},{1,14},{2,13},{3,12},{4,11},{5,10},{6,9},{7,8},{8,7},{9,6},... | collective-permute-start | bytes 24584 | tf_op jit(solution)/shard_map/ppermute | solution.py:106
